TPU v7x, 32 devices: a whole 2x2x4 slice. The times are simulated.
32 devices in a mesh: groups: 2 (over y), tm: 4 (over z), cuts: 2 (over x), col: 2 (over core).
Axes of the slice: x: 2, y: 2, z: 4, core: 2. Of those that a mesh axis runs over, the one named last changes fastest.
Arguments:
- turns: bfloat16 [4096, 4, 1280], P(('groups', 'tm'), 'cuts', 'col'), parts along dimension 0, may hold values from -25 to 25
- shifts: int32 [8], P(('groups', 'tm')), parts along dimension 0, may hold values from -16 to 16
- bands: int32 [8], P(('groups', 'cuts')), parts along dimension 0, may hold values from 2 to 24
- memory: float32 [8], P(('groups', 'cuts')), parts along dimension 0, may hold values from 0.8 to 0.995
Outputs:
- filtered: bfloat16 [8192, 4, 1280], P(('groups', 'tm', 'col'), 'cuts'), parts along dimension 0
There are 2 independent parts, one for each index of `groups`. A program takes and returns all parts, laid end to end along the dimension named above; each array names one. Nothing has to cross between parts.
All inputs are finite; a program needn't handle non-finite values.
Results may differ from a plain program's by a relative error of at most 0.015.
The roundings to bfloat16 on the way count: a program that leaves them out, or rounds other values in their place, can miss the bound.
Values may be sent and summed in bfloat16 or wider, within the bound.
No kernel may reach another device: no remote copies, remote signals or barrier semaphores. Data moves between devices by JAX's collectives and lax.ppermute only.
A program may use at most 64 MiB of HBM per device.

v0:
```python
import math
import jax
import jax.numpy as jnp
from jax import lax
from jax.sharding import PartitionSpec as P

COLUMNS = 1280
BAND_FREQS = 64


def from_behind(block, axis, distance):
    devices = range(lax.axis_size(axis))
    route = [(i - distance, i) for i in devices if i - distance in devices]
    return lax.ppermute(block, axis, route)


def extended(shard, sides, width):
    for axis, dim in sides:
        devices, length = (lax.axis_size(axis), shard.shape[dim])
        up = [(i, (i + 1) % devices) for i in range(devices - 1)]
        down = [(j, i) for i, j in up]
        last = lax.slice_in_dim(shard, length - width, length, axis=dim)
        leading = lax.slice_in_dim(shard, 0, width, axis=dim)
        before = lax.ppermute(last, axis, up)
        after = lax.ppermute(leading, axis, down)
        shard = jnp.concatenate([before, shard, after], axis=dim)
    return shard


def wave_table(angle_count, freq_count):
    freq_index = lax.broadcasted_iota(jnp.int32, (freq_count, angle_count), 0) + 1
    angle_index = lax.broadcasted_iota(jnp.int32, (freq_count, angle_count), 1)
    phase_int = freq_index * angle_index % angle_count
    radians = phase_int.astype(jnp.float32) * (2.0 * math.pi / angle_count)
    return jnp.concatenate([jnp.cos(radians), jnp.sin(radians)], axis=0).astype(jnp.bfloat16)


def damping_weights(bands, freq_count, angle_count):
    freq_values = (jnp.arange(freq_count, dtype=jnp.int32) + 1).astype(jnp.float32)
    band_width = bands.astype(jnp.float32)
    gaussian = jnp.exp(-freq_values[:, None] ** 2 / (2.0 * band_width[None, :] ** 2)) * (
        2.0 / angle_count
    )
    return jnp.concatenate([gaussian, gaussian], axis=0)


def ramp_table(width_total, offset):
    source_col = lax.broadcasted_iota(jnp.int32, (width_total, width_total), 0)
    target_col = lax.broadcasted_iota(jnp.int32, (width_total, width_total), 1)
    lag_index = (target_col - source_col - offset) % width_total
    distance = jnp.minimum(lag_index, width_total - lag_index)
    dist_float = jnp.maximum(distance, 1).astype(jnp.float32)
    tap_value = jnp.where(
        distance == 0, 0.25, jnp.where(distance % 2 == 1, -1.0 / (math.pi**2 * dist_float**2), 0.0)
    )
    return tap_value.astype(jnp.bfloat16)


def local(turns, shifts, bands, memory):
    half_len, row_count, col_width = turns.shape
    angle_count = 2 * half_len
    spread = row_count * col_width
    wave_rows = wave_table(angle_count, BAND_FREQS)
    older_half = from_behind(turns, "tm", 1)
    flat_own = turns.reshape(half_len, spread)
    flat_old = older_half.reshape(half_len, spread)
    window = jnp.concatenate([flat_old, flat_own], axis=0)
    spectrum = jnp.dot(wave_rows, window, preferred_element_type=jnp.float32)
    column_sum = jnp.sum(window, axis=0, dtype=jnp.float32)
    profile = (column_sum / angle_count).reshape(row_count, col_width)
    decay_rate = memory.reshape(row_count, 1)
    tm_count = lax.axis_size("tm")
    tm_index = lax.axis_index("tm")
    lag_steps = tm_index - jnp.arange(tm_count, dtype=jnp.int32)
    lag_float = jnp.maximum(lag_steps, 0).astype(jnp.float32)
    powers = jnp.where(
        lag_steps[:, None] >= 0, jnp.power(decay_rate[:, 0][None, :], lag_float[:, None]), 0.0
    )
    weight = jnp.sum(powers, axis=0)[:, None]
    all_profiles = lax.all_gather(profile, "tm", axis=0, tiled=True)
    stacked = all_profiles.reshape(tm_count, row_count, col_width)
    weighted_sum = jnp.einsum("ur,urc->rc", powers, stacked, precision=lax.Precision.HIGHEST)
    estimate = weighted_sum / weight
    padded = extended(estimate, (("cuts", 0),), 1)
    smooth = (padded[:-2] + 2.0 * padded[1:-1] + padded[2:]) * 0.25
    weights = damping_weights(bands, BAND_FREQS, angle_count)
    scaled = (spectrum.reshape(2 * BAND_FREQS, row_count, col_width) * weights[:, :, None]).astype(
        jnp.bfloat16
    )
    low = jnp.dot(
        wave_rows.T, scaled.reshape(2 * BAND_FREQS, spread), preferred_element_type=jnp.float32
    )
    damped = (window - low - smooth.reshape(1, spread)).astype(jnp.bfloat16)
    damped = damped.reshape(angle_count, row_count, col_width)
    kernel = ramp_table(COLUMNS, shifts[0])
    row_block = lax.all_to_all(damped, "col", split_axis=0, concat_axis=2, tiled=True)
    lead_rows, item_count, full_width = row_block.shape
    result = jnp.dot(
        row_block.reshape(lead_rows * item_count, full_width),
        kernel,
        preferred_element_type=jnp.float32,
    )
    return result.reshape(lead_rows, item_count, full_width).astype(jnp.bfloat16)


def solution(mesh):
    placed = (
        P(("groups", "tm"), "cuts", "col"),
        P(("groups", "tm")),
        P(("groups", "cuts")),
        P(("groups", "cuts")),
    )
    return jax.shard_map(
        local,
        mesh=mesh,
        in_specs=placed,
        out_specs=P(("groups", "tm", "col"), "cuts", None),
        check_vma=False,
    )
```

profile of v0, /device:TPU:0, one launch (start us, length us, event | category | flops | bytes accessed | tf_op | source)
XLA Modules:
  0.0 95.9 jit_solution(11461236508998719598)
XLA Ops:
  0.0 0.0 copy-start.2
  0.0 5.2 %collective-permute-start = (bf16[512,2,640]{2,1,0:T(2,128)(2,1)}, bf16[512,2,640]{2,1,0:T(2,128)(2,1)S(1)}, u32[]{:S(2)}, u32[]{:S(2)}) collective-permute-start(bf16[512,2,640]{2,1,0:T(2,128)(2,1)} %param.4), channel_id=1, source_target_pairs={{0,4},{4,8},{8,12},{1,5},{5,9},{9,13},{2,6},{6,10},{10,14},{3,7},{... | collective-permute-start | bytes 3932168 | tf_op jit(solution)/shard_map/ppermute | solution.py:14
  5.2 2.6 %copy.17 = bf16[64,8,2,640]{3,1,2,0:T(8,128)(2,1)} copy(bf16[64,8,2,640]{3,2,1,0:T(2,128)(2,1)} %bitcast.30) | data formatting | bytes 2621440
  7.8 0.0 copy-done.2
  7.8 0.1 fusion.37
  7.9 0.0 copy-done.1
  7.9 0.2 fusion.49
  8.1 1.2 %cosine_convert_fusion = (bf16[64,1024]{1,0:T(8,128)(2,1)S(1)}, bf16[64,1024]{1,0:T(8,128)(2,1)S(1)}) fusion(s32[64]{0:T(128)S(1)} %iota_add_fusion), kind=kLoop, calls=%fused_computation.41 | loop fusion | flops 1048576 | bytes 262400 | tf_op jit(solution)/shard_map/convert
  9.3 24.1 %collective-permute-done = bf16[512,2,640]{2,1,0:T(2,128)(2,1)S(1)} collective-permute-done((bf16[512,2,640]{2,1,0:T(2,128)(2,1)}, bf16[512,2,640]{2,1,0:T(2,128)(2,1)S(1)}, u32[]{:S(2)}, u32[]{:S(2)}) %collective-permute-start) | collective-permute-done | bytes 1310752 | tf_op jit(solution)/shard_map/ppermute | solution.py:14
  33.4 0.2 copy.16
  33.6 0.1 constant_dynamic-update-slice_fusion.1
  33.7 1.0 %copy-done = bf16[64,8,2,640]{3,1,2,0:T(8,128)(2,1)S(1)} copy-done((bf16[64,8,2,640]{3,1,2,0:T(8,128)(2,1)S(1)}, bf16[64,8,2,640]{3,1,2,0:T(8,128)(2,1)}, u32[]{:S(2)}) %copy-start) | copy-done | bytes 1310744
  34.7 0.1 constant_dynamic-update-slice_fusion
  34.8 0.4 convert_reduce_fusion
  35.3 14.3 %all-gather = f32[4,2,640]{2,1,0:T(2,128)S(1)} all-gather(f32[1,2,640]{2,1,0:T(2,128)S(1)} %reshape.55), channel_id=1, replica_groups=mesh['groups'=2,'tm'=4,'cuts'=2,'col'=2] {'tm'}, dimensions={0}, use_global_device_ids=true | all-gather | bytes 25600 | tf_op jit(solution)/shard_map/all_gather | solution.py:80
  49.5 0.2 fusion.32
  49.7 0.1 bitcast_divide_fusion
  49.8 1.3 %collective-permute-start.2 = (f32[1,640]{1,0:T(1,128)S(1)}, f32[1,640]{1,0:T(1,128)}, u32[]{:S(2)}, u32[]{:S(2)}) collective-permute-start(f32[1,640]{1,0:T(1,128)S(1)} %get-tuple-element.8), channel_id=1, source_target_pairs={{2,0},{3,1},{6,4},{7,5},{10,8},{11,9},{14,12},{15,13},{18,16},{19,... | collective-permute-start | bytes 7688 | tf_op jit(solution)/shard_map/ppermute | solution.py:25
  51.1 5.7 %collective-permute-start.1 = (f32[1,640]{1,0:T(1,128)S(1)}, f32[1,640]{1,0:T(1,128)}, u32[]{:S(2)}, u32[]{:S(2)}) collective-permute-start(f32[1,640]{1,0:T(1,128)S(1)} %get-tuple-element.7), channel_id=1, source_target_pairs={{0,2},{1,3},{4,6},{5,7},{8,10},{9,11},{12,14},{13,15},{16,18},{17,... | collective-permute-start | bytes 7688 | tf_op jit(solution)/shard_map/ppermute | solution.py:24
  56.8 0.1 pad_maximum_fusion.2
  56.8 0.1 copy.10
  57.0 0.2 mul.58
  57.9 0.0 collective-permute-done.2
  57.9 0.0 collective-permute-done.1
  57.9 0.7 fusion.35
  58.6 2.7 %fusion.7 = bf16[1024,1280]{1,0:T(8,128)(2,1)} fusion(bf16[1024,1280]{1,0:T(8,128)(2,1)S(1)} %constant_dynamic-update-slice_fusion, f32[1280]{0:T(1024)S(1)} %sub.42, f32[128,1280]{1,0:T(8,128)S(1)} %bitcast.32, bf16[64,1024]{1,0:T(8,128)(2,1)S(1)} %get-tuple-element.10, bf16[64,1024]{1,0:T(8,128)(2,1)S(1)} %get-tuple-element.9), kind=kOutput, calls=%fused_computation.16 | convolution fusion | flops 677707776 | bytes 6165504 | tf_op jit(solution)/shard_map/dot_general | solution.py:90
  61.3 5.1 %reshape.54 = bf16[1024,2,640]{2,1,0:T(2,128)(2,1)S(1)} reshape(bf16[1024,1280]{1,0:T(8,128)(2,1)} %fusion.7) | data formatting | bytes 5242880 | tf_op jit(solution)/shard_map/reshape | solution.py:94
  66.4 5.8 %all_to_all.15 = bf16[1024,2,640]{2,1,0:T(2,128)(2,1)S(1)} all-to-all(bf16[1024,2,640]{2,1,0:T(2,128)(2,1)S(1)} %reshape.54), channel_id=1, replica_groups=mesh['groups'=2,'tm'=4,'cuts'=2,'col'=2] {'col'}, dimensions={0} | all-to-all | bytes 5242880 | tf_op jit(solution)/shard_map/all_to_all | solution.py:96
  72.2 2.7 %copy.23 = bf16[2,512,2,640]{3,0,1,2:T(2,128)(2,1)S(1)} copy(bf16[2,512,2,640]{3,2,1,0:T(2,128)(2,1)S(1)} %bitcast.25) | data formatting | bytes 5242880 | tf_op jit(solution)/shard_map/all_to_all | solution.py:96
  74.9 2.9 %dot_general.17 = bf16[512,2,1280]{2,0,1:T(8,128)(2,1)} reshape(bf16[512,2,2,640]{3,2,0,1:T(2,128)(2,1)S(1)} %bitcast.26) | data formatting | bytes 5242880 | tf_op jit(solution)/shard_map/dot_general | solution.py:98
  77.9 13.8 %convolution_convert_fusion = bf16[512,2,1280]{2,0,1:T(8,128)(2,1)S(1)} fusion(bf16[512,2,1280]{2,0,1:T(8,128)(2,1)} %dot_general.17, s32[]{:T(128)} %bitcast.24), kind=kOutput, calls=%fused_computation.17 | convolution fusion | flops 3407544320 | bytes 5242884 | tf_op jit(solution)/shard_map/dot_general | solution.py:98
  91.7 4.2 %copy.12 = bf16[512,2,1280]{2,1,0:T(2,128)(2,1)} copy(bf16[512,2,1280]{2,0,1:T(8,128)(2,1)S(1)} %convolution_convert_fusion) | data formatting | bytes 5242880 | tf_op jit(solution)/shard_map/convert_element_type | solution.py:103
  (12 shorter events, 0.1 us)
Async XLA Ops:
  0.0 7.8 %copy-start.2 = (s32[2]{0:T(128)S(1)}, s32[2]{0:T(128)}, u32[]{:S(2)}) copy-start(s32[2]{0:T(128)} %param.6) | copy-start | bytes 28
  0.0 7.9 %copy-start.1 = (f32[2]{0:T(128)S(1)}, f32[2]{0:T(128)}, u32[]{:S(2)}) copy-start(f32[2]{0:T(128)} %param.7) | copy-start | bytes 28
  0.0 33.4 %collective-permute-start = (bf16[512,2,640]{2,1,0:T(2,128)(2,1)}, bf16[512,2,640]{2,1,0:T(2,128)(2,1)S(1)}, u32[]{:S(2)}, u32[]{:S(2)}) collective-permute-start(bf16[512,2,640]{2,1,0:T(2,128)(2,1)} %param.4), channel_id=1, source_target_pairs={{0,4},{4,8},{8,12},{1,5},{5,9},{9,13},{2,6},{6,10},{10,14},{3,7},{... | collective-permute-start | bytes 3932168 | tf_op jit(solution)/shard_map/ppermute | solution.py:14
  33.4 1.3 %copy-start = (bf16[64,8,2,640]{3,1,2,0:T(8,128)(2,1)S(1)}, bf16[64,8,2,640]{3,1,2,0:T(8,128)(2,1)}, u32[]{:S(2)}) copy-start(bf16[64,8,2,640]{3,1,2,0:T(8,128)(2,1)} %copy.17) | copy-start | bytes 3932164
  49.8 8.1 %collective-permute-start.2 = (f32[1,640]{1,0:T(1,128)S(1)}, f32[1,640]{1,0:T(1,128)}, u32[]{:S(2)}, u32[]{:S(2)}) collective-permute-start(f32[1,640]{1,0:T(1,128)S(1)} %get-tuple-element.8), channel_id=1, source_target_pairs={{2,0},{3,1},{6,4},{7,5},{10,8},{11,9},{14,12},{15,13},{18,16},{19,... | collective-permute-start | bytes 7688 | tf_op jit(solution)/shard_map/ppermute | solution.py:25
  51.1 6.8 %collective-permute-start.1 = (f32[1,640]{1,0:T(1,128)S(1)}, f32[1,640]{1,0:T(1,128)}, u32[]{:S(2)}, u32[]{:S(2)}) collective-permute-start(f32[1,640]{1,0:T(1,128)S(1)} %get-tuple-element.7), channel_id=1, source_target_pairs={{0,2},{1,3},{4,6},{5,7},{8,10},{9,11},{12,14},{13,15},{16,18},{17,... | collective-permute-start | bytes 7688 | tf_op jit(solution)/shard_map/ppermute | solution.py:24
where the time goes:
time: 96.3 us; the launch traced here: 95.9 us
  waiting for transfers between devices  24.1 us (25%)
  blocking collectives  20.1 us (21%)
  local copies, waits for them, and re-layouts  19.3 us (20%)
  matrix products  16.6 us (17%)
  starting transfers between devices  12.1 us (13%)
  other arithmetic  2.81 us (3%)
    ppermute x1, waiting for transfers between devices, from_behind(): return lax.ppermute(block, axis, route)  24.1 us
    all_gather x1, blocking collectives, local(): all_profiles = lax.all_gather(profile, 'tm', axis=0, tiled=True)  14.3 us
    dot_general x1, matrix products, local(): jnp.dot(row_block.reshape(lead_rows * item_count, full_width), kernel, pr...  13.8 us
    all_to_all x1, blocking collectives, local(): lax.all_to_all(damped, 'col', split_axis=0, concat_axis=2, tiled=True)  5.84 us
    ppermute x1, starting transfers between devices, extended(): before = lax.ppermute(last, axis, up)  5.68 us
    ppermute x1, starting transfers between devices, from_behind(): return lax.ppermute(block, axis, route)  5.16 us
    reshape x1, local copies, waits for them, and re-layouts, local(): damped = damped.reshape(angle_count, row_count, col_width)  5.07 us
    convert_element_type x1, local copies, waits for them, and re-layouts, local(): result.reshape(lead_rows, item_count, full_width).astype(jnp.bfloat16)  4.19 us
  transfers between devices with their start and end apart: 3, of which 1 were waited for; matrix products, arithmetic and copies ran while one was open for 5% of the time, Pallas kernels for 0%

commit v1 on v0

--- a/solution.py
+++ b/solution.py
@@ -93,7 +93,10 @@
     damped = (window - low - smooth.reshape(1, spread)).astype(jnp.bfloat16)
     damped = damped.reshape(angle_count, row_count, col_width)
     kernel = ramp_table(COLUMNS, shifts[0])
-    row_block = lax.all_to_all(damped, "col", split_axis=0, concat_axis=2, tiled=True)
+    row_block = jnp.concatenate(
+        lax.all_to_all(jnp.stack(jnp.split(damped, lax.axis_size("col"), axis=0)), "col", 0, 0),
+        axis=2,
+    )
     lead_rows, item_count, full_width = row_block.shape
     result = jnp.dot(
         row_block.reshape(lead_rows * item_count, full_width),

time: 96.3 us -> 104 us (1.080)
  other arithmetic: 2.81 us -> 8.06 us
  local copies, waits for them, and re-layouts: 19.3 us -> 21.4 us
    another operation x1 -> x2, other arithmetic: 1.23 us -> 6.47 us  [the longest x1 5.24 us: local(): jnp.stack(jnp.split(damped, lax.axis_size('col'), axis=0))]
    another operation x0 -> x2, local copies, waits for them, and re-layouts: none -> 4.19 us  [local(): jnp.stack(jnp.split(damped, lax.axis_size('col'), axis=0))]
    split x0 -> x1, local copies, waits for them, and re-layouts: none -> 2.95 us  [local(): jnp.split(damped, lax.axis_size('col'), axis=0)]
    all_to_all x1 -> x0, local copies, waits for them, and re-layouts: 2.7 us -> none  [local(): lax.all_to_all(damped, 'col', split_axis=0, concat_axis=2, tiled=True)]
    reshape x1, local copies, waits for them, and re-layouts: 5.07 us -> 2.7 us  [local(): jnp.concatenate(lax.all_to_all(jnp.stack(jnp.split(damped, lax.axis_size(...]
  transfers between devices with their start and end apart: 3 -> 3, of which waited for: 1 -> 1; matrix products, arithmetic and copies ran while one was open for 5% -> 4% of each run, Pallas kernels for 0% -> 0%
where the time goes in v1:
time: 104 us; the launch traced here: 103 us
  waiting for transfers between devices  24.1 us (23%)
  local copies, waits for them, and re-layouts  21.4 us (21%)
  blocking collectives  20.1 us (19%)
  matrix products  16.6 us (16%)
  starting transfers between devices  12.2 us (12%)
  other arithmetic  8.06 us (8%)
    ppermute x1, waiting for transfers between devices, from_behind(): return lax.ppermute(block, axis, route)  24.1 us
    all_gather x1, blocking collectives, local(): all_profiles = lax.all_gather(profile, 'tm', axis=0, tiled=True)  14.3 us
    dot_general x1, matrix products, local(): jnp.dot(row_block.reshape(lead_rows * item_count, full_width), kernel, pr...  13.8 us
    all_to_all x1, blocking collectives, local(): lax.all_to_all(jnp.stack(jnp.split(damped, lax.axis_size('col'), axis=0))...  5.84 us
    ppermute x1, starting transfers between devices, extended(): before = lax.ppermute(last, axis, up)  5.71 us
    another operation x1, other arithmetic, local(): jnp.stack(jnp.split(damped, lax.axis_size('col'), axis=0))  5.24 us
    ppermute x1, starting transfers between devices, from_behind(): return lax.ppermute(block, axis, route)  5.16 us
    another operation x2, local copies, waits for them, and re-layouts, local(): jnp.stack(jnp.split(damped, lax.axis_size('col'), axis=0))  4.19 us
  transfers between devices with their start and end apart: 3, of which 1 were waited for; matrix products, arithmetic and copies ran while one was open for 4% of the time, Pallas kernels for 0%

profile of v1, /device:TPU:0, one launch (start us, length us, event | category | flops | bytes accessed | tf_op | source)
XLA Modules:
  0.0 103.2 jit_solution(11423649982785886773)
XLA Ops:
  0.0 5.2 %collective-permute-start = (bf16[512,2,640]{2,1,0:T(2,128)(2,1)}, bf16[512,2,640]{2,1,0:T(2,128)(2,1)S(1)}, u32[]{:S(2)}, u32[]{:S(2)}) collective-permute-start(bf16[512,2,640]{2,1,0:T(2,128)(2,1)} %param.4), channel_id=1, source_target_pairs={{0,4},{4,8},{8,12},{1,5},{5,9},{9,13},{2,6},{6,10},{10,14},{3,7},{... | collective-permute-start | bytes 3932168 | tf_op jit(solution)/shard_map/ppermute | solution.py:14
  5.2 2.6 %copy.17 = bf16[64,8,2,640]{3,1,2,0:T(8,128)(2,1)} copy(bf16[64,8,2,640]{3,2,1,0:T(2,128)(2,1)} %bitcast.26) | data formatting | bytes 2621440
  7.8 0.1 fusion.37
  7.9 0.2 fusion.49
  8.1 1.2 %cosine_convert_fusion = (bf16[64,1024]{1,0:T(8,128)(2,1)S(1)}, bf16[64,1024]{1,0:T(8,128)(2,1)S(1)}) fusion(s32[64]{0:T(128)S(1)} %iota_add_fusion), kind=kLoop, calls=%fused_computation.41 | loop fusion | flops 1048576 | bytes 262400 | tf_op jit(solution)/shard_map/convert
  9.3 24.1 %collective-permute-done = bf16[512,2,640]{2,1,0:T(2,128)(2,1)S(1)} collective-permute-done((bf16[512,2,640]{2,1,0:T(2,128)(2,1)}, bf16[512,2,640]{2,1,0:T(2,128)(2,1)S(1)}, u32[]{:S(2)}, u32[]{:S(2)}) %collective-permute-start) | collective-permute-done | bytes 1310752 | tf_op jit(solution)/shard_map/ppermute | solution.py:14
  33.4 0.2 copy.16
  33.6 0.1 constant_dynamic-update-slice_fusion.1
  33.7 1.0 copy-done
  34.7 0.1 constant_dynamic-update-slice_fusion
  34.8 0.4 convert_reduce_fusion
  35.3 14.3 %all-gather = f32[4,2,640]{2,1,0:T(2,128)S(1)} all-gather(f32[1,2,640]{2,1,0:T(2,128)S(1)} %reshape.58), channel_id=1, replica_groups=mesh['groups'=2,'tm'=4,'cuts'=2,'col'=2] {'tm'}, dimensions={0}, use_global_device_ids=true | all-gather | bytes 25600 | tf_op jit(solution)/shard_map/all_gather | solution.py:80
  49.5 0.2 fusion.32
  49.7 0.1 bitcast_divide_fusion
  49.8 1.3 %collective-permute-start.2 = (f32[1,640]{1,0:T(1,128)S(1)}, f32[1,640]{1,0:T(1,128)}, u32[]{:S(2)}, u32[]{:S(2)}) collective-permute-start(f32[1,640]{1,0:T(1,128)S(1)} %get-tuple-element.10), channel_id=1, source_target_pairs={{2,0},{3,1},{6,4},{7,5},{10,8},{11,9},{14,12},{15,13},{18,16},{19,... | collective-permute-start | bytes 7688 | tf_op jit(solution)/shard_map/ppermute | solution.py:25
  51.1 5.7 %collective-permute-start.1 = (f32[1,640]{1,0:T(1,128)S(1)}, f32[1,640]{1,0:T(1,128)}, u32[]{:S(2)}, u32[]{:S(2)}) collective-permute-start(f32[1,640]{1,0:T(1,128)S(1)} %get-tuple-element.9), channel_id=1, source_target_pairs={{0,2},{1,3},{4,6},{5,7},{8,10},{9,11},{12,14},{13,15},{16,18},{17,... | collective-permute-start | bytes 7688 | tf_op jit(solution)/shard_map/ppermute | solution.py:24
  56.8 0.1 pad_maximum_fusion.3
  56.9 0.1 copy.10
  57.0 0.2 mul.58
  57.9 0.0 collective-permute-done.2
  57.9 0.0 collective-permute-done.1
  57.9 0.7 fusion.35
  58.7 2.7 %fusion.7 = bf16[1024,1280]{1,0:T(8,128)(2,1)} fusion(bf16[1024,1280]{1,0:T(8,128)(2,1)S(1)} %constant_dynamic-update-slice_fusion, f32[1280]{0:T(1024)S(1)} %sub.42, f32[128,1280]{1,0:T(8,128)S(1)} %bitcast.28, bf16[64,1024]{1,0:T(8,128)(2,1)S(1)} %get-tuple-element.12, bf16[64,1024]{1,0:T(8,128)(2,1)S(1)} %get-tuple-element.11), kind=kOutput, calls=%fused_computation.16 | convolution fusion | flops 677707776 | bytes 6165504 | tf_op jit(solution)/shard_map/dot_general | solution.py:90
  61.4 3.0 %fusion.50 = (bf16[512,1280]{1,0:T(8,128)(2,1)S(1)}, bf16[512,1280]{1,0:T(8,128)(2,1)}) fusion(bf16[1024,1280]{1,0:T(8,128)(2,1)} %fusion.7), kind=kLoop, calls=%fused_computation.76 | loop fusion | bytes 5242880 | tf_op jit(solution)/shard_map/split | solution.py:97
  64.3 3.0 %stack.10 = bf16[1,512,2,640]{3,2,1,0:T(2,128)(2,1)S(1)} reshape(bf16[512,1280]{1,0:T(8,128)(2,1)} %get-tuple-element.8) | data formatting | bytes 2621440 | tf_op jit(solution)/shard_map/stack | solution.py:97
  67.3 1.2 %stack.9 = bf16[1,512,2,640]{3,2,1,0:T(2,128)(2,1)} reshape(bf16[512,1280]{1,0:T(8,128)(2,1)S(1)} %get-tuple-element.7) | data formatting | bytes 2621440 | tf_op jit(solution)/shard_map/stack | solution.py:97
  68.5 5.2 %pad_maximum_fusion = bf16[2,512,2,640]{3,2,1,0:T(2,128)(2,1)S(1)} fusion(bf16[1,512,2,640]{3,2,1,0:T(2,128)(2,1)S(1)} %stack.10, bf16[1,512,2,640]{3,2,1,0:T(2,128)(2,1)} %stack.9), kind=kLoop, calls=%fused_computation.28 | loop fusion | flops 1310720 | bytes 5242880 | tf_op jit(solution)/shard_map/stack | solution.py:97
  73.8 5.8 %all_to_all.5 = bf16[2,512,2,640]{3,2,1,0:T(2,128)(2,1)S(1)} all-to-all(bf16[2,512,2,640]{3,2,1,0:T(2,128)(2,1)S(1)} %pad_maximum_fusion), channel_id=1, replica_groups=mesh['groups'=2,'tm'=4,'cuts'=2,'col'=2] {'col'}, dimensions={0} | all-to-all | bytes 5242880 | tf_op jit(solution)/shard_map/all_to_all | solution.py:97
  79.6 2.7 %copy.11 = bf16[512,2,2,640]{3,2,0,1:T(2,128)(2,1)S(1)} copy(bf16[512,2,2,640]{3,1,0,2:T(2,128)(2,1)S(1)} %bitcast.22) | data formatting | bytes 5242880 | tf_op jit(solution)/shard_map/reshape | solution.py:96
  82.3 2.9 %dot_general.17 = bf16[512,2,1280]{2,0,1:T(8,128)(2,1)} reshape(bf16[512,2,2,640]{3,2,0,1:T(2,128)(2,1)S(1)} %copy.11) | data formatting | bytes 5242880 | tf_op jit(solution)/shard_map/dot_general | solution.py:101
  85.3 13.8 %convolution_convert_fusion = bf16[512,2,1280]{2,0,1:T(8,128)(2,1)S(1)} fusion(bf16[512,2,1280]{2,0,1:T(8,128)(2,1)} %dot_general.17, s32[]{:T(128)} %bitcast.21), kind=kOutput, calls=%fused_computation.17 | convolution fusion | flops 3407544320 | bytes 5242884 | tf_op jit(solution)/shard_map/dot_general | solution.py:101
  99.0 4.2 %copy.12 = bf16[512,2,1280]{2,1,0:T(2,128)(2,1)} copy(bf16[512,2,1280]{2,0,1:T(8,128)(2,1)S(1)} %convolution_convert_fusion) | data formatting | bytes 5242880 | tf_op jit(solution)/shard_map/convert_element_type | solution.py:106
  (15 shorter events, 0.1 us)
Async XLA Ops:
  0.0 7.8 %copy-start.2 = (s32[2]{0:T(128)S(1)}, s32[2]{0:T(128)}, u32[]{:S(2)}) copy-start(s32[2]{0:T(128)} %param.6) | copy-start | bytes 28
  0.0 7.9 %copy-start.1 = (f32[2]{0:T(128)S(1)}, f32[2]{0:T(128)}, u32[]{:S(2)}) copy-start(f32[2]{0:T(128)} %param.7) | copy-start | bytes 28
  0.0 33.4 %collective-permute-start = (bf16[512,2,640]{2,1,0:T(2,128)(2,1)}, bf16[512,2,640]{2,1,0:T(2,128)(2,1)S(1)}, u32[]{:S(2)}, u32[]{:S(2)}) collective-permute-start(bf16[512,2,640]{2,1,0:T(2,128)(2,1)} %param.4), channel_id=1, source_target_pairs={{0,4},{4,8},{8,12},{1,5},{5,9},{9,13},{2,6},{6,10},{10,14},{3,7},{... | collective-permute-start | bytes 3932168 | tf_op jit(solution)/shard_map/ppermute | solution.py:14
  33.4 1.3 %copy-start = (bf16[64,8,2,640]{3,1,2,0:T(8,128)(2,1)S(1)}, bf16[64,8,2,640]{3,1,2,0:T(8,128)(2,1)}, u32[]{:S(2)}) copy-start(bf16[64,8,2,640]{3,1,2,0:T(8,128)(2,1)} %copy.17) | copy-start | bytes 3932164
  49.8 8.1 %collective-permute-start.2 = (f32[1,640]{1,0:T(1,128)S(1)}, f32[1,640]{1,0:T(1,128)}, u32[]{:S(2)}, u32[]{:S(2)}) collective-permute-start(f32[1,640]{1,0:T(1,128)S(1)} %get-tuple-element.10), channel_id=1, source_target_pairs={{2,0},{3,1},{6,4},{7,5},{10,8},{11,9},{14,12},{15,13},{18,16},{19,... | collective-permute-start | bytes 7688 | tf_op jit(solution)/shard_map/ppermute | solution.py:25
  51.1 6.9 %collective-permute-start.1 = (f32[1,640]{1,0:T(1,128)S(1)}, f32[1,640]{1,0:T(1,128)}, u32[]{:S(2)}, u32[]{:S(2)}) collective-permute-start(f32[1,640]{1,0:T(1,128)S(1)} %get-tuple-element.9), channel_id=1, source_target_pairs={{0,2},{1,3},{4,6},{5,7},{8,10},{9,11},{12,14},{13,15},{16,18},{17,... | collective-permute-start | bytes 7688 | tf_op jit(solution)/shard_map/ppermute | solution.py:24
